TPU v7x, 256 devices: a whole 4x4x8 slice. The times are simulated.
256 devices in a mesh: ctx: 16 (over x, y_hi, core), chan: 16 (over z, y_lo).
Axes of the slice: x: 4, y: 4 (y_hi: 2, y_lo: 2; y = y_hi * 2 + y_lo), z: 8, core: 2. Of those that a mesh axis runs over, the one named last changes fastest.
Arguments:
- inputs: bfloat16 [256, 4096], P('ctx', 'chan'), may hold values from -6 to 6
- gain: float32 [4096], replicated, may hold values from 0.25 to 1.75
- w_in: bfloat16 [4096, 3, 4096], P(None, None, 'chan'), may hold values from -0.09375 to 0.09375
- w_out: bfloat16 [4096, 4096], P('chan'), may hold values from -0.125 to 0.125
- history: bfloat16 [4096, 2, 4096], P('ctx', None, 'chan'), may hold values from -6 to 6
- filt_far: bfloat16 [4096, 2, 4096], P('ctx', None, 'chan'), may hold values from -0.09375 to 0.09375
- filt_near: bfloat16 [256, 2, 4096], P(None, None, 'chan'), may hold values from -0.09375 to 0.09375
Outputs:
- mixed: bfloat16 [256, 4096], P('ctx', 'chan')
- gated: bfloat16 [256, 4096], P('ctx', 'chan')
All inputs are finite; a program needn't handle non-finite values.
Results may differ from a plain program's by a relative error of at most 0.0066.
Values may be sent and summed in bfloat16 or wider, within the bound.
No kernel may reach another device: no remote copies, remote signals or barrier semaphores. Data moves between devices by JAX's collectives and lax.ppermute only.
A program may use at most 64 MiB of HBM per device.

v0:
```python
import jax
import jax.numpy as jnp
import numpy as np
from jax import lax
from jax.experimental import pallas as pl
from jax.experimental.pallas import tpu as pltpu
from jax.sharding import PartitionSpec as P

BF16 = jnp.bfloat16
F32 = jnp.float32
VMEM = pl.BlockSpec(memory_space=pltpu.VMEM)
SMEM = pl.BlockSpec(memory_space=pltpu.SMEM)
HBM = pl.BlockSpec(memory_space=pltpu.HBM)
LIMIT = 24 << 20


def split_up(table):
    high = np.asarray(table, np.float32).astype(jnp.bfloat16)
    low = (table - high.astype(np.float64)).astype(np.float32).astype(jnp.bfloat16)
    return high, low


def dft_tables(length):
    order = np.concatenate([np.arange(0, length, 2), np.arange(1, length, 2)])
    theta = np.pi * (order + 0.5) / length
    angle = theta[:, None] * np.arange(length)[None, :]
    forward = np.concatenate([np.cos(angle), np.sin(angle)], 0)
    back = theta[None, :] * (length - 1 - np.arange(length))[:, None]
    inverse = np.concatenate([np.cos(back), -np.sin(back)], 1) / length
    return *split_up(forward), *split_up(inverse)


def dot(a, b):
    return jnp.dot(a, b, preferred_element_type=F32)


def spectrum(forward, rows):
    half = forward[0].shape[0] // 2
    return [sum(dot(table[r], rows) for table in forward) for r in (slice(half), slice(half, None))]


def back_to_time(inverse, product):
    upper = product.astype(BF16)
    lower = (product - upper.astype(F32)).astype(BF16)
    high, low = inverse
    half = high.shape[0] // 2
    return jnp.concatenate(
        [
            dot(high[r], upper) + dot(high[r], lower) + dot(low[r], upper)
            for r in (slice(half), slice(half, None))
        ],
        0,
    )


def halves(rows):
    half = rows.shape[0] // 2
    return rows[:half], rows[half:]


def near_to_time(high, product):
    upper = product.astype(BF16)
    lower = (product - upper.astype(F32)).astype(BF16)
    lanes = product.shape[1]
    both = dot(high, jnp.concatenate([upper, lower], 1))
    return both[:, :lanes] + both[:, lanes:]


def times_conjugate(window, signal):
    (wc, ws), (sc, ss) = window, signal
    return jnp.concatenate([wc * sc + ws * ss, wc * ss - ws * sc], 0)


def spread_out(rows, spread):
    count, kinds, width = rows.shape
    flat = rows[...].reshape(count * kinds, width)
    lanes = spread.shape[2]
    for h in range(width // lanes):
        spread[h] = flat[:, h * lanes : (h + 1) * lanes].astype(F32)


def parted(spread, kinds, which):
    count = spread.shape[1] // kinds
    rows = [spread[h, pl.ds(which, count, stride=kinds), :].astype(BF16) for h in range(spread.shape[0])]
    return jnp.concatenate(rows, 1)


def past_part(own, after, history, f, i):
    quarter = f[0].shape[0] // 4
    first_cos, first_sin = spectrum(f, own)
    bc, bs = spectrum(f, after)
    window = (
        first_cos + jnp.concatenate([-bs[:quarter], bs[quarter:]], 0),
        first_sin + jnp.concatenate([bc[:quarter], -bc[quarter:]], 0),
    )
    return back_to_time(i, times_conjugate(window, spectrum(f, history)))


def open_kernel(*refs):
    (inputs, *loads), (copies, *kept), (held, sems) = refs[:9], refs[9:18], refs[18:]
    moves = [pltpu.make_async_copy(a, b, sems.at[n]) for n, (a, b) in enumerate(zip([inputs, *loads], [held, *kept]))]
    for move in moves:
        move.start()
    moves[0].wait()
    count = copies.shape[0]
    sent = [pltpu.make_async_copy(held, copies.at[d], sems.at[len(moves) + d]) for d in range(count)]
    for move in sent:
        move.start()
    for move in moves[1:] + sent:
        move.wait()


def first_past_kernel(
    index, last, border, own, near, history, fh, fl, ih, il, w_hbm, keep, send, later, w_head, spread, sem
):
    load = pltpu.make_async_copy(w_hbm.at[0, pl.ds(0, w_head.shape[0]), :], w_head, sem)
    load.start()

    @pl.when(last[0] > 0)
    def _():
        spread_out(near, spread.at[1])

    @pl.when(last[0] == 0)
    def _():
        spread_out(border, spread.at[1])

    spread_out(own, spread.at[0])
    spread_out(history, spread.at[2])
    part = past_part(*(parted(spread.at[n], 2, 0) for n in range(3)), (fh, fl), (ih, il))
    lanes = keep.shape[1]
    low, high = part[:, :lanes], part[:, lanes:]
    mine = index[0] % 2
    keep[...] = jnp.where(mine == 0, low, high)
    send[...] = jnp.where(mine == 0, high, low)
    for n in range(3):
        later[n] = parted(spread.at[n], 2, 1)
    load.wait()


def second_past_kernel(index, rows, fh, fl, ih, il, keep, send, parts):
    mine = index[0] % 2
    parts[...] = past_part(rows[0], rows[1], rows[2], (fh, fl), (ih, il)).reshape(parts.shape)
    half, lanes = keep.shape[0] // 2, keep.shape[1]
    for h in range(2):
        there = pl.ds(h * half, half)
        span = slice(h * lanes, (h + 1) * lanes)
        keep[there] = parts[:, mine, :, span].reshape(half, lanes)
        send[there] = parts[:, 1 - mine, :, span].reshape(half, lanes)


def project_kernel(gathered, gain, w_head, w_hbm, keep, came, out_hbm, gate_two, out, normed, w, sems, done):
    pieces, rows, width = gathered.shape
    depth = pieces * width
    ready = w_head.shape[0]
    step = depth // 4
    chunks = []
    for k in range(3):
        edges = [*range(ready, depth, step), depth] if k == 0 else range(0, depth + 1, step)
        chunks += [(k, a, b) for a, b in zip(edges, edges[1:])]
    copies = []
    for n, (k, a, b) in enumerate(chunks):
        span = pl.ds(a, b - a)
        copies.append(pltpu.make_async_copy(w_hbm.at[k, span, :], w.at[k, span, :], sems.at[n]))
        copies[-1].start()
    lanes = out.shape[2]
    fresh = keep.shape[0]
    pair = (keep[...] + came[...]).astype(BF16)
    for d in range(out.shape[0]):
        start = (d % 2) * (fresh // 2) + (d // 2) * rows
        out[d, 2 * rows :] = pair[start : start + rows]
    total = jnp.zeros((rows, width), F32)
    for s in range(pieces):
        x = gathered[s].astype(F32)
        total += x * x
    mean_sq = jnp.sum(total, axis=1, keepdims=True) / depth
    scale = lax.rsqrt(mean_sq + 1e-06)
    for s in range(pieces):
        g = jnp.concatenate([gain[2 * s : 2 * s + 1], gain[2 * s + 1 : 2 * s + 2]], 1)
        normed[:, s * width : (s + 1) * width] = (gathered[s].astype(F32) * scale * g).astype(BF16)
    sums = [dot(normed[:, :ready], w_head[...]), jnp.zeros((rows, width), F32), jnp.zeros((rows, width), F32)]
    sent = pltpu.make_async_copy(out, out_hbm, done)
    for n, (k, a, b) in enumerate(chunks):
        copies[n].wait()
        sums[k] += dot(normed[:, a:b], w[k, a:b, :])
        if k < 2 and b == depth:
            part = sums[k].astype(BF16)
            for d in range(out.shape[0]):
                out[d, k * rows : (k + 1) * rows] = part[:, (d % 2) * lanes : (d % 2 + 1) * lanes]
            if k == 1:
                sent.start()
    gate_two[...] = sums[2].astype(BF16)
    sent.wait()


def near_kernel(index, near_hbm, f, w_hbm, spectra, w_out, near, spread, sems):
    first = pltpu.make_async_copy(near_hbm, near, sems.at[0])
    first.start()
    load = pltpu.make_async_copy(w_hbm, w_out, sems.at[1])
    load.start()
    first.wait()
    lanes = spectra.shape[2]
    half = pl.ds(pl.multiple_of((index[0] % 2) * lanes, lanes), lanes)
    spread_out(near.at[:, :, half], spread)
    for which in range(2):
        half = spectra.shape[1] // 2
        spectra[which, :half], spectra[which, half:] = spectrum((f,), parted(spread, 2, which))
    load.wait()


def mix_kernel(index, arrived, here, there, spectra, f, i, keep, send, gated_all, sums):
    count, packed, lanes = arrived.shape
    rows = packed // 3
    fresh = count * rows
    values = arrived[:, :rows].reshape(fresh, lanes)
    gate_one = arrived[:, rows : 2 * rows].reshape(fresh, lanes).astype(F32)
    past_one = here[...].astype(F32) + there[...].astype(F32)
    first = near_to_time(i[...], times_conjugate(halves(spectra[0]), halves(dot(f[...], values))))
    gated = (gate_one * (past_one + first)).astype(BF16)
    gated_all[...] = gated
    mine = index[0] % 2
    chip = pl.ds(pl.multiple_of((index[0] - mine) * rows, 2 * rows), 2 * rows)
    second = near_to_time(i[chip, :], times_conjugate(halves(spectra[1]), halves(dot(f[...], gated))))
    past_two = [arrived[p, 2 * rows :].astype(F32) for p in range(2)]
    for s in range(2, count):
        past_two[s % 2] += arrived[s, 2 * rows :].astype(F32)
    sums[0] = (second + jnp.concatenate(past_two, 0)).reshape(sums.shape[1:])
    sums[1] = gated_all[chip, :].astype(F32).reshape(sums.shape[1:])
    keep[...] = sums[:, mine]
    send[...] = sums[:, 1 - mine]


def finish_kernel(index, keep, came, gate_two, w_out, partial, gated):
    first = index[0] % 2 == 0
    low, high = jnp.where(first, keep[...], came[...]), jnp.where(first, came[...], keep[...])
    both = jnp.concatenate([low, high], 2)
    gated[...] = both[1].astype(BF16)
    mixed_in = (gate_two[...].astype(F32) * both[0]).astype(BF16)
    width = partial.shape[2]
    for d in range(partial.shape[0]):
        partial[d] = dot(mixed_in, w_out[:, d * width : (d + 1) * width]).astype(BF16)


def total_kernel(arrived, out):
    out[...] = jnp.sum(arrived[...].astype(F32), axis=0).astype(BF16)


def call(kernel, out_shape, in_specs, flops, nbytes, scratch=(), limit=LIMIT, out_specs=None):
    return pl.pallas_call(
        kernel,
        out_shape=out_shape,
        in_specs=in_specs,
        out_specs=out_specs or jax.tree.map(lambda _: VMEM, out_shape),
        scratch_shapes=list(scratch),
        cost_estimate=pl.CostEstimate(flops=flops, bytes_accessed=nbytes, transcendentals=0),
        compiler_params=pltpu.CompilerParams(vmem_limit_bytes=limit),
    )


def in_hbm(array):
    return pltpu.with_memory_space_constraint(array, pltpu.HBM)


def exchanged(array, axis):
    return lax.all_to_all(array, axis, split_axis=0, concat_axis=0, tiled=True)


def swapped(array, axis, step):
    return lax.ppermute(array, axis, [(i, i ^ step) for i in range(lax.axis_size(axis))])


def added(a, b):
    return (a.astype(F32) + b.astype(F32)).astype(BF16)


def layer(inputs, gain, w_in, w_out, history, filt_far, filt_near):
    rows, width = inputs.shape
    fresh = filt_near.shape[0]
    ctx_count = lax.axis_size("ctx")
    chan_count = lax.axis_size("chan")
    ctx_index = lax.axis_index("ctx")
    tables = [jnp.asarray(t) for t in dft_tables(fresh)]
    index = ctx_index.reshape(1).astype(jnp.int32)
    last = (index == ctx_count - 1).astype(jnp.int32)

    unit = fresh * fresh * 4 * width
    w_three = w_in.transpose(1, 0, 2)
    border = lax.ppermute(filt_far, "ctx", [(i, i - 1) for i in range(1, ctx_count)])
    loads = (filt_far, filt_near, history, *tables, gain.reshape(-1, 128))
    copies, own, near, past, fh, fl, ih, il, scales = call(
        open_kernel,
        (
            jax.ShapeDtypeStruct((chan_count, rows, width), BF16),
            *(jax.ShapeDtypeStruct(a.shape, a.dtype) for a in loads),
        ),
        [HBM] * 9,
        1 << 10,
        1 << 21,
        scratch=[pltpu.VMEM((rows, width), BF16), pltpu.SemaphoreType.DMA((9 + chan_count,))],
        out_specs=(pl.BlockSpec(memory_space=pl.ANY), *[VMEM] * 8),
    )(*(in_hbm(a) for a in (inputs, *loads)))
    gathered = exchanged(copies, "chan")

    lanes = width // 2
    half = jax.ShapeDtypeStruct((fresh, lanes), F32)
    spread = (2 * fresh, lanes)
    head = jax.ShapeDtypeStruct((9 * width, width), BF16)
    keep_one, send_one, later, w_head = call(
        first_past_kernel,
        (half, half, jax.ShapeDtypeStruct((3, fresh, width), BF16), head),
        [SMEM, SMEM] + [VMEM] * 8 + [HBM],
        unit * 9,
        2 << 20,
        scratch=[pltpu.VMEM((3, 2, *spread), F32), pltpu.SemaphoreType.DMA],
    )(index, last, border, own, near, past, fh, fl, ih, il, in_hbm(w_three))
    came_one = swapped(send_one, "ctx", 1)
    keep_two, send_two = call(
        second_past_kernel,
        (half, half),
        [SMEM] + [VMEM] * 5,
        unit * 9,
        1 << 20,
        scratch=[pltpu.VMEM((ctx_count // 2, 2, rows, width), F32)],
    )(index, later, fh, fl, ih, il)
    came_two = swapped(send_two, "ctx", 1)
    here = added(keep_one, came_one)
    there = swapped(here, "ctx", 8)

    payload, gate_two = call(
        project_kernel,
        (
            jax.ShapeDtypeStruct((ctx_count, 3 * rows, lanes), BF16),
            jax.ShapeDtypeStruct((rows, width), BF16),
        ),
        [VMEM, VMEM, VMEM, HBM, VMEM, VMEM],
        2 * rows * w_in.size,
        2 * w_in.size,
        scratch=[
            pltpu.VMEM((ctx_count, 3 * rows, lanes), BF16),
            pltpu.VMEM((rows, w_in.shape[0]), BF16),
            pltpu.VMEM(w_three.shape, BF16),
            pltpu.SemaphoreType.DMA((10,)),
            pltpu.SemaphoreType.DMA,
        ],
        out_specs=(pl.BlockSpec(memory_space=pl.ANY), VMEM),
    )(gathered, scales, w_head, in_hbm(w_three), keep_two, came_two)

    here = added(here, there)
    payload, here = lax.optimization_barrier((payload, here))
    there = swapped(here, "ctx", 2)
    arrived = exchanged(payload, "ctx")
    here = added(here, there)
    there = swapped(here, "ctx", 4)
    spectra, w_out = call(
        near_kernel,
        (jax.ShapeDtypeStruct((2, 2 * fresh, lanes), F32), jax.ShapeDtypeStruct(w_out.shape, BF16)),
        [SMEM, HBM, VMEM, HBM],
        unit * 2,
        2 << 20,
        scratch=[pltpu.VMEM(filt_near.shape, BF16), pltpu.VMEM((1, *spread), F32), pltpu.SemaphoreType.DMA((2,))],
    )(index, in_hbm(filt_near), fh, in_hbm(w_out))

    block = jax.ShapeDtypeStruct((2, rows, lanes), F32)
    keep, send = call(
        mix_kernel,
        (block, block),
        [SMEM] + [VMEM] * 6,
        unit * 4,
        4 << 20,
        scratch=[
            pltpu.VMEM((fresh, lanes), BF16),
            pltpu.VMEM((2, 2, rows, lanes), F32),
        ],
    )(index, arrived, here, there, spectra, fh, ih)
    came = swapped(send, "ctx", 1)
    partial, gated = call(
        finish_kernel,
        (
            jax.ShapeDtypeStruct((chan_count, rows, width), BF16),
            jax.ShapeDtypeStruct((rows, width), BF16),
        ),
        [SMEM] + [VMEM] * 4,
        unit,
        1 << 20,
    )(index, keep, came, gate_two, w_out)
    mixed = call(
        total_kernel, jax.ShapeDtypeStruct((rows, width), BF16), [VMEM], 1 << 16, 1 << 17
    )(exchanged(partial, "chan"))
    return (mixed, gated)


def solution(mesh):
    placed = (
        P("ctx", "chan"),
        P(),
        P(None, None, "chan"),
        P("chan", None),
        P("ctx", None, "chan"),
        P("ctx", None, "chan"),
        P(None, None, "chan"),
    )
    return jax.shard_map(
        layer,
        mesh=mesh,
        in_specs=placed,
        out_specs=(P("ctx", "chan"), P("ctx", "chan")),
        check_vma=False,
    )
```

profile of v0, /device:TPU:1, one launch (start us, length us, event | category | flops | bytes accessed | tf_op | source)
XLA Modules:
  0.0 68.8 jit_solution(15224104778361736508)
XLA Ops:
  0.6 5.1 %collective-permute-start = (bf16[256,2,256]{2,1,0:T(2,128)(2,1)}, bf16[256,2,256]{2,1,0:T(2,128)(2,1)S(1)}, u32[]{:S(2)}, u32[]{:S(2)}) collective-permute-start(bf16[256,2,256]{2,1,0:T(2,128)(2,1)} %refs_1_.1), channel_id=1, source_target_pairs={{16,0},{32,16},{48,32},{64,48},{80,64},{96,80},{112,96},{128,112},... | collective-permute-start | bytes 786440 | tf_op jit(solution)/shard_map/ppermute | solution.py:287
  5.7 1.7 %shard_map.122 = (bf16[16,16,256]{2,1,0:T(8,128)(2,1)}, bf16[256,2,256]{2,1,0:T(2,128)(2,1)S(1)}, bf16[256,2,256]{2,1,0:T(2,128)(2,1)S(1)}, bf16[256,2,256]{2,1,...) custom-call(bf16[16,256]{1,0:T(8,128)(2,1)} %refs_0_.1, ...), custom_call_target="tpu_custom_call" | custom-call | flops 1024 | bytes 2097152 | tf_op jit(solution)/shard_map/pallas_call | solution.py:289
  7.5 3.6 %collective-permute-done.border = bf16[256,2,256]{2,1,0:T(2,128)(2,1)S(1)} collective-permute-done((bf16[256,2,256]{2,1,0:T(2,128)(2,1)}, bf16[256,2,256]{2,1,0:T(2,128)(2,1)S(1)}, u32[]{:S(2)}, u32[]{:S(2)}) %collective-permute-start) | collective-permute-done | bytes 262176 | tf_op jit(solution)/shard_map/ppermute | solution.py:287
  11.1 2.2 %shard_map.123 = (f32[256,128]{1,0:T(8,128)S(1)}, f32[256,128]{1,0:T(8,128)}, bf16[3,256,256]{2,1,0:T(8,128)(2,1)S(1)}, bf16[2304,256]{1,0:T(8,128)(2,1)S(1)}) custom-call(s32[1]{0:T(128)} %bitcast.index, s32[1]{0:T(128)S(6)} %convert_element_type.24.last, bf16[256,2,256]{2,1,0:T(2,128)(2,1)S(1)} %collective-permute-done.border, ...), custom_call_target="tpu_custom_call" | custom-call | flops 603979776 | bytes 2097152 | tf_op jit(solution)/shard_map/pallas_call | solution.py:307
  13.3 0.0 copy-start
  13.3 0.7 %copy-done = bf16[3,256,256]{2,1,0:T(8,128)(2,1)} copy-done((bf16[3,256,256]{2,1,0:T(8,128)(2,1)}, bf16[3,256,256]{2,1,0:T(8,128)(2,1)S(1)}, u32[]{:S(2)}) %copy-start) | copy-done | bytes 393240
  14.0 0.0 collective-permute-start.2
  14.0 9.1 %all-to-all-start = ((bf16[16,16,256]{2,1,0:T(8,128)(2,1)}), bf16[16,16,256]{2,1,0:T(8,128)(2,1)S(1)}, u32[]{:S(2)}, u32[]{:S(2)}) async-start(bf16[16,16,256]{2,1,0:T(8,128)(2,1)} %get-tuple-element.27), calls=%async_computation | async-start | bytes 262144 | tf_op jit(solution)/shard_map/all_to_all | solution.py:264
  23.1 0.0 copy-start.1
  23.1 1.0 %copy-done.1 = bf16[3,256,256]{2,1,0:T(8,128)(2,1)S(1)} copy-done((bf16[3,256,256]{2,1,0:T(8,128)(2,1)S(1)}, bf16[3,256,256]{2,1,0:T(8,128)(2,1)}, u32[]{:S(2)}) %copy-start.1) | copy-done | bytes 393240
  24.1 1.0 %shard_map.124 = (f32[256,128]{1,0:T(8,128)S(1)}, f32[256,128]{1,0:T(8,128)S(1)}) custom-call(s32[1]{0:T(128)} %bitcast.index, bf16[3,256,256]{2,1,0:T(8,128)(2,1)S(1)} %copy-done.1, bf16[512,256]{1,0:T(8,128)(2,1)S(1)} %get-tuple-element.32.fh.f, bf16[512,256]{1,0:T(8,128)(2,1)S(1)} %get-tuple-element.33.fl, bf16[256,512]{1,0:T(8,128)(2,1)S(1)} %get-tuple-element.34.ih.i, ...), custom_call_target="tpu_custom_call" | custom-call | flops 603979776 | bytes 1048576 | tf_op jit(solution)/shard_map/pallas_call | solution.py:316
  25.1 0.9 %collective-permute-start.1 = (f32[256,128]{1,0:T(8,128)S(1)}, f32[256,128]{1,0:T(8,128)S(1)}, u32[]{:S(2)}, u32[]{:S(2)}) collective-permute-start(f32[256,128]{1,0:T(8,128)S(1)} %get-tuple-element.39), channel_id=1, source_target_pairs={{0,16},{16,0},{32,48},{48,32},{64,80},{80,64},{96,112},{112,96},{1... | collective-permute-start | bytes 393224 | tf_op jit(solution)/shard_map/ppermute | solution.py:268
  25.9 0.0 collective-permute-done.2
  26.0 2.8 %collective-permute-start.3 = (bf16[256,128]{1,0:T(8,128)(2,1)S(1)}, bf16[256,128]{1,0:T(8,128)(2,1)S(1)}, u32[]{:S(2)}, u32[]{:S(2)}) collective-permute-start(bf16[256,128]{1,0:T(8,128)(2,1)S(1)} %add_convert_fusion.2), channel_id=1, source_target_pairs={{0,128},{16,144},{32,160},{48,176},{64,192},{80,208},{96,224},{112... | collective-permute-start | bytes 196616 | tf_op jit(solution)/shard_map/ppermute | solution.py:268
  28.8 2.8 %all-to-all-done.gathered = bf16[16,16,256]{2,1,0:T(8,128)(2,1)S(1)} async-done(((bf16[16,16,256]{2,1,0:T(8,128)(2,1)}), bf16[16,16,256]{2,1,0:T(8,128)(2,1)S(1)}, u32[]{:S(2)}, u32[]{:S(2)}) %all-to-all-start) | async-done | bytes 131104 | tf_op jit(solution)/shard_map/all_to_all | solution.py:264
  31.5 0.0 collective-permute-done.1.came
  31.6 3.1 %shard_map.125 = (bf16[16,48,128]{2,1,0:T(8,128)(2,1)}, bf16[16,256]{1,0:T(8,128)(2,1)S(1)}) custom-call(bf16[16,16,256]{2,1,0:T(8,128)(2,1)S(1)} %all-to-all-done.gathered, f32[32,128]{1,0:T(8,128)S(1)} %get-tuple-element.28.gain, bf16[2304,256]{1,0:T(8,128)(2,1)S(1)} %get-tuple-element.36.w_head, bf16[3,4096,256]{2,1,0:T(8,128)(2,1)} %bitcast.4, ...), custom_call_target="tpu_custom_call" | custom-call | flops 100663296 | bytes 6291456 | tf_op jit(solution)/shard_map/pallas_call | solution.py:328
  34.7 0.0 collective-permute-done.3
  34.7 3.6 %collective-permute-start.4 = (bf16[256,128]{1,0:T(8,128)(2,1)S(1)}, bf16[256,128]{1,0:T(8,128)(2,1)S(1)}, u32[]{:S(2)}, u32[]{:S(2)}) collective-permute-start(bf16[256,128]{1,0:T(8,128)(2,1)S(1)} %add_convert_fusion.1), channel_id=1, source_target_pairs={{0,32},{16,48},{32,0},{48,16},{64,96},{80,112},{96,64},{112,80},{1... | collective-permute-start | bytes 196616 | tf_op jit(solution)/shard_map/ppermute | solution.py:268
  38.3 6.7 %all-to-all-start.1 = ((bf16[16,48,128]{2,1,0:T(8,128)(2,1)}), bf16[16,48,128]{2,1,0:T(8,128)(2,1)S(1)}, u32[]{:S(2)}, u32[]{:S(2)}) async-start(bf16[16,48,128]{2,1,0:T(8,128)(2,1)} %get-tuple-element.43), calls=%async_computation.1 | async-start | bytes 393216 | tf_op jit(solution)/shard_map/all_to_all | solution.py:264
  45.0 0.0 collective-permute-done.4
  45.1 1.4 %collective-permute-start.5 = (bf16[256,128]{1,0:T(8,128)(2,1)S(1)}, bf16[256,128]{1,0:T(8,128)(2,1)S(1)}, u32[]{:S(2)}, u32[]{:S(2)}) collective-permute-start(bf16[256,128]{1,0:T(8,128)(2,1)S(1)} %add_convert_fusion.here), channel_id=1, source_target_pairs={{0,64},{16,80},{32,96},{48,112},{64,0},{80,16},{96,32},{112,48},{1... | collective-permute-start | bytes 196616 | tf_op jit(solution)/shard_map/ppermute | solution.py:268
  46.5 1.7 %shard_map.126 = (f32[2,512,128]{2,1,0:T(8,128)S(1)}, bf16[256,4096]{1,0:T(8,128)(2,1)S(1)}) custom-call(s32[1]{0:T(128)} %bitcast.index, bf16[256,2,256]{2,1,0:T(2,128)(2,1)} %near_hbm.1, bf16[512,256]{1,0:T(8,128)(2,1)S(1)} %get-tuple-element.32.fh.f, bf16[256,4096]{1,0:T(8,128)(2,1)} %w_hbm.1), custom_call_target="tpu_custom_call" | custom-call | flops 134217728 | bytes 2097152 | tf_op jit(solution)/shard_map/pallas_call | solution.py:353
  48.2 2.5 %collective-permute-done.5.there = bf16[256,128]{1,0:T(8,128)(2,1)S(1)} collective-permute-done((bf16[256,128]{1,0:T(8,128)(2,1)S(1)}, bf16[256,128]{1,0:T(8,128)(2,1)S(1)}, u32[]{:S(2)}, u32[]{:S(2)}) %collective-permute-start.5) | collective-permute-done | bytes 65568 | tf_op jit(solution)/shard_map/ppermute | solution.py:268
  50.8 2.8 %all-to-all-done.1.arrived = bf16[16,48,128]{2,1,0:T(8,128)(2,1)S(1)} async-done(((bf16[16,48,128]{2,1,0:T(8,128)(2,1)}), bf16[16,48,128]{2,1,0:T(8,128)(2,1)S(1)}, u32[]{:S(2)}, u32[]{:S(2)}) %all-to-all-start.1) | async-done | bytes 196640 | tf_op jit(solution)/shard_map/all_to_all | solution.py:264
  53.6 0.9 %shard_map.127 = (f32[2,16,128]{2,1,0:T(8,128)S(1)}, f32[2,16,128]{2,1,0:T(8,128)S(1)}) custom-call(s32[1]{0:T(128)} %bitcast.index, bf16[16,48,128]{2,1,0:T(8,128)(2,1)S(1)} %all-to-all-done.1.arrived, bf16[256,128]{1,0:T(8,128)(2,1)S(1)} %add_convert_fusion.here, bf16[256,128]{1,0:T(8,128)(2,1)S(1)} %collective-permute-done.5.there, ...), custom_call_target="tpu_custom_call" | custom-call | flops 268435456 | bytes 4194304 | tf_op jit(solution)/shard_map/pallas_call | solution.py:363
  54.5 0.2 collective-permute-start.6
  54.7 1.1 %collective-permute-done.6.came = f32[2,16,128]{2,1,0:T(8,128)S(1)} collective-permute-done((f32[2,16,128]{2,1,0:T(8,128)S(1)}, f32[2,16,128]{2,1,0:T(8,128)S(1)}, u32[]{:S(2)}, u32[]{:S(2)}) %collective-permute-start.6) | collective-permute-done | bytes 16416 | tf_op jit(solution)/shard_map/ppermute | solution.py:268
  55.8 0.9 %shard_map.128 = (bf16[16,16,256]{2,1,0:T(8,128)(2,1)S(1)}, bf16[16,256]{1,0:T(8,128)(2,1)}) custom-call(s32[1]{0:T(128)} %bitcast.index, f32[2,16,128]{2,1,0:T(8,128)S(1)} %get-tuple-element.46.keep, f32[2,16,128]{2,1,0:T(8,128)S(1)} %collective-permute-done.6.came, bf16[16,256]{1,0:T(8,128)(2,1)S(1)} %get-tuple-element.48.gate_two, ...), custom_call_target="tpu_custom_call" | custom-call | flops 67108864 | bytes 1048576 | tf_op jit(solution)/shard_map/pallas_call | solution.py:375
  56.7 11.5 %all_to_all.15.arrived = bf16[16,16,256]{2,1,0:T(8,128)(2,1)S(1)} all-to-all(bf16[16,16,256]{2,1,0:T(8,128)(2,1)S(1)} %get-tuple-element.50), channel_id=1, replica_groups=mesh['ctx'=16,'chan'=16] {'chan'}, dimensions={0} | all-to-all | bytes 262144 | tf_op jit(solution)/shard_map/all_to_all | solution.py:264
  68.1 0.6 shard_map.129
  (3 shorter events, 0.1 us)
Async XLA Ops:
  0.6 10.5 %collective-permute-start = (bf16[256,2,256]{2,1,0:T(2,128)(2,1)}, bf16[256,2,256]{2,1,0:T(2,128)(2,1)S(1)}, u32[]{:S(2)}, u32[]{:S(2)}) collective-permute-start(bf16[256,2,256]{2,1,0:T(2,128)(2,1)} %refs_1_.1), channel_id=1, source_target_pairs={{16,0},{32,16},{48,32},{64,48},{80,64},{96,80},{112,96},{128,112},... | collective-permute-start | bytes 786440 | tf_op jit(solution)/shard_map/ppermute | solution.py:287
  13.3 0.7 %copy-start = (bf16[3,256,256]{2,1,0:T(8,128)(2,1)}, bf16[3,256,256]{2,1,0:T(8,128)(2,1)S(1)}, u32[]{:S(2)}) copy-start(bf16[3,256,256]{2,1,0:T(8,128)(2,1)S(1)} %get-tuple-element.37.rows) | copy-start | bytes 1179652
  14.0 11.9 %collective-permute-start.2 = (f32[256,128]{1,0:T(8,128)}, f32[256,128]{1,0:T(8,128)S(1)}, u32[]{:S(2)}, u32[]{:S(2)}) collective-permute-start(f32[256,128]{1,0:T(8,128)} %get-tuple-element.42), channel_id=1, source_target_pairs={{0,16},{16,0},{32,48},{48,32},{64,80},{80,64},{96,112},{112,96},{1... | collective-permute-start | bytes 393224 | tf_op jit(solution)/shard_map/ppermute | solution.py:268
  14.0 17.5 %all-to-all-start = ((bf16[16,16,256]{2,1,0:T(8,128)(2,1)}), bf16[16,16,256]{2,1,0:T(8,128)(2,1)S(1)}, u32[]{:S(2)}, u32[]{:S(2)}) async-start(bf16[16,16,256]{2,1,0:T(8,128)(2,1)} %get-tuple-element.27), calls=%async_computation | async-start | bytes 262144 | tf_op jit(solution)/shard_map/all_to_all | solution.py:264
  23.1 1.0 %copy-start.1 = (bf16[3,256,256]{2,1,0:T(8,128)(2,1)S(1)}, bf16[3,256,256]{2,1,0:T(8,128)(2,1)}, u32[]{:S(2)}) copy-start(bf16[3,256,256]{2,1,0:T(8,128)(2,1)} %copy-done) | copy-start | bytes 1179652
  25.1 6.5 %collective-permute-start.1 = (f32[256,128]{1,0:T(8,128)S(1)}, f32[256,128]{1,0:T(8,128)S(1)}, u32[]{:S(2)}, u32[]{:S(2)}) collective-permute-start(f32[256,128]{1,0:T(8,128)S(1)} %get-tuple-element.39), channel_id=1, source_target_pairs={{0,16},{16,0},{32,48},{48,32},{64,80},{80,64},{96,112},{112,96},{1... | collective-permute-start | bytes 393224 | tf_op jit(solution)/shard_map/ppermute | solution.py:268
  26.0 8.7 %collective-permute-start.3 = (bf16[256,128]{1,0:T(8,128)(2,1)S(1)}, bf16[256,128]{1,0:T(8,128)(2,1)S(1)}, u32[]{:S(2)}, u32[]{:S(2)}) collective-permute-start(bf16[256,128]{1,0:T(8,128)(2,1)S(1)} %add_convert_fusion.2), channel_id=1, source_target_pairs={{0,128},{16,144},{32,160},{48,176},{64,192},{80,208},{96,224},{112... | collective-permute-start | bytes 196616 | tf_op jit(solution)/shard_map/ppermute | solution.py:268
  34.7 10.3 %collective-permute-start.4 = (bf16[256,128]{1,0:T(8,128)(2,1)S(1)}, bf16[256,128]{1,0:T(8,128)(2,1)S(1)}, u32[]{:S(2)}, u32[]{:S(2)}) collective-permute-start(bf16[256,128]{1,0:T(8,128)(2,1)S(1)} %add_convert_fusion.1), channel_id=1, source_target_pairs={{0,32},{16,48},{32,0},{48,16},{64,96},{80,112},{96,64},{112,80},{1... | collective-permute-start | bytes 196616 | tf_op jit(solution)/shard_map/ppermute | solution.py:268
  38.3 15.2 %all-to-all-start.1 = ((bf16[16,48,128]{2,1,0:T(8,128)(2,1)}), bf16[16,48,128]{2,1,0:T(8,128)(2,1)S(1)}, u32[]{:S(2)}, u32[]{:S(2)}) async-start(bf16[16,48,128]{2,1,0:T(8,128)(2,1)} %get-tuple-element.43), calls=%async_computation.1 | async-start | bytes 393216 | tf_op jit(solution)/shard_map/all_to_all | solution.py:264
  45.1 5.7 %collective-permute-start.5 = (bf16[256,128]{1,0:T(8,128)(2,1)S(1)}, bf16[256,128]{1,0:T(8,128)(2,1)S(1)}, u32[]{:S(2)}, u32[]{:S(2)}) collective-permute-start(bf16[256,128]{1,0:T(8,128)(2,1)S(1)} %add_convert_fusion.here), channel_id=1, source_target_pairs={{0,64},{16,80},{32,96},{48,112},{64,0},{80,16},{96,32},{112,48},{1... | collective-permute-start | bytes 196616 | tf_op jit(solution)/shard_map/ppermute | solution.py:268
  54.5 1.3 %collective-permute-start.6 = (f32[2,16,128]{2,1,0:T(8,128)S(1)}, f32[2,16,128]{2,1,0:T(8,128)S(1)}, u32[]{:S(2)}, u32[]{:S(2)}) collective-permute-start(f32[2,16,128]{2,1,0:T(8,128)S(1)} %get-tuple-element.47), channel_id=1, source_target_pairs={{0,16},{16,0},{32,48},{48,32},{64,80},{80,64},{96,112},{112,96},{1... | collective-permute-start | bytes 49160 | tf_op jit(solution)/shard_map/ppermute | solution.py:268
where the time goes:
time: 69.2 us; the launch traced here: 68.8 us
  starting transfers between devices  29.8 us (43%)
  waiting for transfers between devices  12.9 us (19%)
  Pallas kernels  12.1 us (17%)
  blocking collectives  11.5 us (17%)
  local copies, waits for them, and re-layouts  1.73 us (2%)
  between operations  0.75 us (1%)
    all_to_all x2, starting transfers between devices, exchanged(): return lax.all_to_all(array, axis, split_axis=0, concat_axis=0, tiled=True)  15.7 us
    all_to_all x1, blocking collectives, exchanged(): return lax.all_to_all(array, axis, split_axis=0, concat_axis=0, tiled=True)  11.5 us
    ppermute x6, starting transfers between devices, swapped(): lax.ppermute(array, axis, [(i, i ^ step) for i in range(lax.axis_size(axi...  8.93 us
    all_to_all x2, waiting for transfers between devices, exchanged(): return lax.all_to_all(array, axis, split_axis=0, concat_axis=0, tiled=True)  5.59 us
    ppermute x1, starting transfers between devices, layer(): lax.ppermute(filt_far, 'ctx', [(i, i - 1) for i in range(1, ctx_count)])  5.11 us
    ppermute x6, waiting for transfers between devices, swapped(): lax.ppermute(array, axis, [(i, i ^ step) for i in range(lax.axis_size(axi...  3.65 us
    ppermute x1, waiting for transfers between devices, layer(): lax.ppermute(filt_far, 'ctx', [(i, i - 1) for i in range(1, ctx_count)])  3.63 us
    pallas_call x1, Pallas kernels, layer(): call(project_kernel, (jax.ShapeDtypeStruct((ctx_count, 3 * rows, lanes),...  3.14 us
  transfers between devices with their start and end apart: 9, of which 5 were waited for; matrix products, arithmetic and copies ran while one was open for 0% of the time, Pallas kernels for 11%

commit v1 on v0

--- a/solution.py
+++ b/solution.py
@@ -42,11 +42,10 @@
 def back_to_time(inverse, product):
     upper = product.astype(BF16)
     lower = (product - upper.astype(F32)).astype(BF16)
-    high, low = inverse
-    half = high.shape[0] // 2
+    half = inverse.shape[0] // 2
     return jnp.concatenate(
         [
-            dot(high[r], upper) + dot(high[r], lower) + dot(low[r], upper)
+            dot(inverse[r], upper) + dot(inverse[r], lower)
             for r in (slice(half), slice(half, None))
         ],
         0,
@@ -97,7 +96,7 @@
 
 
 def open_kernel(*refs):
-    (inputs, *loads), (copies, *kept), (held, sems) = refs[:9], refs[9:18], refs[18:]
+    (inputs, *loads), (copies, *kept), (held, sems) = refs[:8], refs[8:16], refs[16:]
     moves = [pltpu.make_async_copy(a, b, sems.at[n]) for n, (a, b) in enumerate(zip([inputs, *loads], [held, *kept]))]
     for move in moves:
         move.start()
@@ -111,7 +110,7 @@
 
 
 def first_past_kernel(
-    index, last, border, own, near, history, fh, fl, ih, il, w_hbm, keep, send, later, w_head, spread, sem
+    index, last, border, own, near, history, fh, fl, ih, w_hbm, keep, send, later, w_head, spread, sem
 ):
     load = pltpu.make_async_copy(w_hbm.at[0, pl.ds(0, w_head.shape[0]), :], w_head, sem)
     load.start()
@@ -126,7 +125,7 @@
 
     spread_out(own, spread.at[0])
     spread_out(history, spread.at[2])
-    part = past_part(*(parted(spread.at[n], 2, 0) for n in range(3)), (fh, fl), (ih, il))
+    part = past_part(*(parted(spread.at[n], 2, 0) for n in range(3)), (fh, fl), ih)
     lanes = keep.shape[1]
     low, high = part[:, :lanes], part[:, lanes:]
     mine = index[0] % 2
@@ -137,9 +136,9 @@
     load.wait()
 
 
-def second_past_kernel(index, rows, fh, fl, ih, il, keep, send, parts):
+def second_past_kernel(index, rows, fh, fl, ih, keep, send, parts):
     mine = index[0] % 2
-    parts[...] = past_part(rows[0], rows[1], rows[2], (fh, fl), (ih, il)).reshape(parts.shape)
+    parts[...] = past_part(rows[0], rows[1], rows[2], (fh, fl), ih).reshape(parts.shape)
     half, lanes = keep.shape[0] // 2, keep.shape[1]
     for h in range(2):
         there = pl.ds(h * half, half)
@@ -278,7 +277,7 @@
     ctx_count = lax.axis_size("ctx")
     chan_count = lax.axis_size("chan")
     ctx_index = lax.axis_index("ctx")
-    tables = [jnp.asarray(t) for t in dft_tables(fresh)]
+    tables = [jnp.asarray(t) for t in dft_tables(fresh)[:3]]
     index = ctx_index.reshape(1).astype(jnp.int32)
     last = (index == ctx_count - 1).astype(jnp.int32)
 
@@ -286,17 +285,17 @@
     w_three = w_in.transpose(1, 0, 2)
     border = lax.ppermute(filt_far, "ctx", [(i, i - 1) for i in range(1, ctx_count)])
     loads = (filt_far, filt_near, history, *tables, gain.reshape(-1, 128))
-    copies, own, near, past, fh, fl, ih, il, scales = call(
+    copies, own, near, past, fh, fl, ih, scales = call(
         open_kernel,
         (
             jax.ShapeDtypeStruct((chan_count, rows, width), BF16),
             *(jax.ShapeDtypeStruct(a.shape, a.dtype) for a in loads),
         ),
-        [HBM] * 9,
+        [HBM] * 8,
         1 << 10,
         1 << 21,
-        scratch=[pltpu.VMEM((rows, width), BF16), pltpu.SemaphoreType.DMA((9 + chan_count,))],
-        out_specs=(pl.BlockSpec(memory_space=pl.ANY), *[VMEM] * 8),
+        scratch=[pltpu.VMEM((rows, width), BF16), pltpu.SemaphoreType.DMA((8 + chan_count,))],
+        out_specs=(pl.BlockSpec(memory_space=pl.ANY), *[VMEM] * 7),
     )(*(in_hbm(a) for a in (inputs, *loads)))
     gathered = exchanged(copies, "chan")
 
@@ -307,23 +306,23 @@
     keep_one, send_one, later, w_head = call(
         first_past_kernel,
         (half, half, jax.ShapeDtypeStruct((3, fresh, width), BF16), head),
-        [SMEM, SMEM] + [VMEM] * 8 + [HBM],
+        [SMEM, SMEM] + [VMEM] * 7 + [HBM],
         unit * 9,
         2 << 20,
         scratch=[pltpu.VMEM((3, 2, *spread), F32), pltpu.SemaphoreType.DMA],
-    )(index, last, border, own, near, past, fh, fl, ih, il, in_hbm(w_three))
+    )(index, last, border, own, near, past, fh, fl, ih, in_hbm(w_three))
     came_one = swapped(send_one, "ctx", 1)
     keep_two, send_two = call(
         second_past_kernel,
         (half, half),
-        [SMEM] + [VMEM] * 5,
+        [SMEM] + [VMEM] * 4,
         unit * 9,
         1 << 20,
         scratch=[pltpu.VMEM((ctx_count // 2, 2, rows, width), F32)],
-    )(index, later, fh, fl, ih, il)
+    )(index, later, fh, fl, ih)
     came_two = swapped(send_two, "ctx", 1)
     here = added(keep_one, came_one)
-    there = swapped(here, "ctx", 8)
+    there = swapped(here, "ctx", 2)
 
     payload, gate_two = call(
         project_kernel,
@@ -346,7 +345,7 @@
 
     here = added(here, there)
     payload, here = lax.optimization_barrier((payload, here))
-    there = swapped(here, "ctx", 2)
+    there = swapped(here, "ctx", 8)
     arrived = exchanged(payload, "ctx")
     here = added(here, there)
     there = swapped(here, "ctx", 4)

time: 69.2 us -> 69.1 us (level)
  starting transfers between devices: 29.8 us -> 31.1 us
  Pallas kernels: 12.1 us -> 11.2 us
    all_to_all x2, starting transfers between devices: 15.7 us -> 17.1 us  [exchanged(): return lax.all_to_all(array, axis, split_axis=0, concat_axis=0, tiled=True)]
    pallas_call x1, Pallas kernels: 2.15 us -> 1.44 us  [layer(): call(first_past_kernel, (half, half, jax.ShapeDtypeStruct((3, fresh, widt...]
    all_to_all x2, waiting for transfers between devices: 5.59 us -> 4.89 us  [exchanged(): return lax.all_to_all(array, axis, split_axis=0, concat_axis=0, tiled=True)]
where the time goes in v1:
time: 69.1 us; the launch traced here: 68.7 us
  starting transfers between devices  31.1 us (45%)
  waiting for transfers between devices  12.3 us (18%)
  blocking collectives  11.5 us (17%)
  Pallas kernels  11.2 us (16%)
  local copies, waits for them, and re-layouts  1.73 us (3%)
  between operations  0.75 us (1%)
    all_to_all x2, starting transfers between devices, exchanged(): return lax.all_to_all(array, axis, split_axis=0, concat_axis=0, tiled=True)  17.1 us
    all_to_all x1, blocking collectives, exchanged(): return lax.all_to_all(array, axis, split_axis=0, concat_axis=0, tiled=True)  11.5 us
    ppermute x6, starting transfers between devices, swapped(): lax.ppermute(array, axis, [(i, i ^ step) for i in range(lax.axis_size(axi...  8.93 us
    ppermute x1, starting transfers between devices, layer(): lax.ppermute(filt_far, 'ctx', [(i, i - 1) for i in range(1, ctx_count)])  5.11 us
    all_to_all x2, waiting for transfers between devices, exchanged(): return lax.all_to_all(array, axis, split_axis=0, concat_axis=0, tiled=True)  4.89 us
    ppermute x1, waiting for transfers between devices, layer(): lax.ppermute(filt_far, 'ctx', [(i, i - 1) for i in range(1, ctx_count)])  3.72 us
    ppermute x6, waiting for transfers between devices, swapped(): lax.ppermute(array, axis, [(i, i ^ step) for i in range(lax.axis_size(axi...  3.65 us
    pallas_call x1, Pallas kernels, layer(): call(project_kernel, (jax.ShapeDtypeStruct((ctx_count, 3 * rows, lanes),...  3.14 us
  transfers between devices with their start and end apart: 9, of which 5 were waited for; matrix products, arithmetic and copies ran while one was open for 0% of the time, Pallas kernels for 11%

profile of v1, /device:TPU:1, one launch (start us, length us, event | category | flops | bytes accessed | tf_op | source)
XLA Modules:
  0.0 68.7 jit_solution(8956672888819082892)
XLA Ops:
  0.6 5.1 %collective-permute-start = (bf16[256,2,256]{2,1,0:T(2,128)(2,1)}, bf16[256,2,256]{2,1,0:T(2,128)(2,1)S(1)}, u32[]{:S(2)}, u32[]{:S(2)}) collective-permute-start(bf16[256,2,256]{2,1,0:T(2,128)(2,1)} %refs_1_.1), channel_id=1, source_target_pairs={{16,0},{32,16},{48,32},{64,48},{80,64},{96,80},{112,96},{128,112},... | collective-permute-start | bytes 786440 | tf_op jit(solution)/shard_map/ppermute | solution.py:286
  5.7 1.6 %shard_map.113 = (bf16[16,16,256]{2,1,0:T(8,128)(2,1)}, bf16[256,2,256]{2,1,0:T(2,128)(2,1)S(1)}, bf16[256,2,256]{2,1,0:T(2,128)(2,1)S(1)}, bf16[256,2,256]{2,1,...) custom-call(bf16[16,256]{1,0:T(8,128)(2,1)} %refs_0_.1, ...), custom_call_target="tpu_custom_call" | custom-call | flops 1024 | bytes 2097152 | tf_op jit(solution)/shard_map/pallas_call | solution.py:288
  7.4 3.7 %collective-permute-done.border = bf16[256,2,256]{2,1,0:T(2,128)(2,1)S(1)} collective-permute-done((bf16[256,2,256]{2,1,0:T(2,128)(2,1)}, bf16[256,2,256]{2,1,0:T(2,128)(2,1)S(1)}, u32[]{:S(2)}, u32[]{:S(2)}) %collective-permute-start) | collective-permute-done | bytes 262176 | tf_op jit(solution)/shard_map/ppermute | solution.py:286
  11.1 1.4 %shard_map.114 = (f32[256,128]{1,0:T(8,128)S(1)}, f32[256,128]{1,0:T(8,128)S(1)}, bf16[3,256,256]{2,1,0:T(8,128)(2,1)S(1)}, bf16[2304,256]{1,0:T(8,128)(2,1)S(1)}) custom-call(s32[1]{0:T(128)} %bitcast.index, s32[1]{0:T(128)S(6)} %convert_element_type.24.last, bf16[256,2,256]{2,1,0:T(2,128)(2,1)S(1)} %collective-permute-done.border, ...), custom_call_target="tpu_custom_call" | custom-call | flops 603979776 | bytes 2097152 | tf_op jit(solution)/shard_map/pallas_call | solution.py:306
  12.5 0.0 copy-start
  12.6 0.7 %copy-done = bf16[3,256,256]{2,1,0:T(8,128)(2,1)} copy-done((bf16[3,256,256]{2,1,0:T(8,128)(2,1)}, bf16[3,256,256]{2,1,0:T(8,128)(2,1)S(1)}, u32[]{:S(2)}) %copy-start) | copy-done | bytes 393240
  13.3 0.0 collective-permute-start.2
  13.3 9.1 %all-to-all-start = ((bf16[16,16,256]{2,1,0:T(8,128)(2,1)}), bf16[16,16,256]{2,1,0:T(8,128)(2,1)S(1)}, u32[]{:S(2)}, u32[]{:S(2)}) async-start(bf16[16,16,256]{2,1,0:T(8,128)(2,1)} %get-tuple-element.26), calls=%async_computation | async-start | bytes 262144 | tf_op jit(solution)/shard_map/all_to_all | solution.py:263
  22.4 0.0 copy-start.1
  22.4 1.0 %copy-done.1 = bf16[3,256,256]{2,1,0:T(8,128)(2,1)S(1)} copy-done((bf16[3,256,256]{2,1,0:T(8,128)(2,1)S(1)}, bf16[3,256,256]{2,1,0:T(8,128)(2,1)}, u32[]{:S(2)}) %copy-start.1) | copy-done | bytes 393240
  23.4 0.9 %shard_map.115 = (f32[256,128]{1,0:T(8,128)S(1)}, f32[256,128]{1,0:T(8,128)S(1)}) custom-call(s32[1]{0:T(128)} %bitcast.index, bf16[3,256,256]{2,1,0:T(8,128)(2,1)S(1)} %copy-done.1, bf16[512,256]{1,0:T(8,128)(2,1)S(1)} %get-tuple-element.31.fh.f, bf16[512,256]{1,0:T(8,128)(2,1)S(1)} %get-tuple-element.32.fl, bf16[256,512]{1,0:T(8,128)(2,1)S(1)} %get-tuple-element.33.ih.i), custom_call_target="tpu_custom_call" | custom-call | flops 603979776 | bytes 1048576 | tf_op jit(solution)/shard_map/pallas_call | solution.py:315
  24.3 0.9 %collective-permute-start.1 = (f32[256,128]{1,0:T(8,128)S(1)}, f32[256,128]{1,0:T(8,128)S(1)}, u32[]{:S(2)}, u32[]{:S(2)}) collective-permute-start(f32[256,128]{1,0:T(8,128)S(1)} %get-tuple-element.37), channel_id=1, source_target_pairs={{0,16},{16,0},{32,48},{48,32},{64,80},{80,64},{96,112},{112,96},{1... | collective-permute-start | bytes 393224 | tf_op jit(solution)/shard_map/ppermute | solution.py:267
  25.1 0.0 collective-permute-done.2
  25.2 3.6 %collective-permute-start.3 = (bf16[256,128]{1,0:T(8,128)(2,1)S(1)}, bf16[256,128]{1,0:T(8,128)(2,1)S(1)}, u32[]{:S(2)}, u32[]{:S(2)}) collective-permute-start(bf16[256,128]{1,0:T(8,128)(2,1)S(1)} %add_convert_fusion.2), channel_id=1, source_target_pairs={{0,32},{16,48},{32,0},{48,16},{64,96},{80,112},{96,64},{112,80},{1... | collective-permute-start | bytes 196616 | tf_op jit(solution)/shard_map/ppermute | solution.py:267
  28.8 2.1 %all-to-all-done.gathered = bf16[16,16,256]{2,1,0:T(8,128)(2,1)S(1)} async-done(((bf16[16,16,256]{2,1,0:T(8,128)(2,1)}), bf16[16,16,256]{2,1,0:T(8,128)(2,1)S(1)}, u32[]{:S(2)}, u32[]{:S(2)}) %all-to-all-start) | async-done | bytes 131104 | tf_op jit(solution)/shard_map/all_to_all | solution.py:263
  30.8 0.0 collective-permute-done.1.came
  30.8 3.1 %shard_map.116 = (bf16[16,48,128]{2,1,0:T(8,128)(2,1)}, bf16[16,256]{1,0:T(8,128)(2,1)S(1)}) custom-call(bf16[16,16,256]{2,1,0:T(8,128)(2,1)S(1)} %all-to-all-done.gathered, f32[32,128]{1,0:T(8,128)S(1)} %get-tuple-element.27.gain, bf16[2304,256]{1,0:T(8,128)(2,1)S(1)} %get-tuple-element.34.w_head, bf16[3,4096,256]{2,1,0:T(8,128)(2,1)} %bitcast.4, ...), custom_call_target="tpu_custom_call" | custom-call | flops 100663296 | bytes 6291456 | tf_op jit(solution)/shard_map/pallas_call | solution.py:327
  34.0 0.0 collective-permute-done.3
  34.0 2.8 %collective-permute-start.4 = (bf16[256,128]{1,0:T(8,128)(2,1)S(1)}, bf16[256,128]{1,0:T(8,128)(2,1)S(1)}, u32[]{:S(2)}, u32[]{:S(2)}) collective-permute-start(bf16[256,128]{1,0:T(8,128)(2,1)S(1)} %add_convert_fusion.1), channel_id=1, source_target_pairs={{0,128},{16,144},{32,160},{48,176},{64,192},{80,208},{96,224},{112... | collective-permute-start | bytes 196616 | tf_op jit(solution)/shard_map/ppermute | solution.py:267
  36.9 8.0 %all-to-all-start.1 = ((bf16[16,48,128]{2,1,0:T(8,128)(2,1)}), bf16[16,48,128]{2,1,0:T(8,128)(2,1)S(1)}, u32[]{:S(2)}, u32[]{:S(2)}) async-start(bf16[16,48,128]{2,1,0:T(8,128)(2,1)} %get-tuple-element.41), calls=%async_computation.1 | async-start | bytes 393216 | tf_op jit(solution)/shard_map/all_to_all | solution.py:263
  44.9 0.0 collective-permute-done.4
  44.9 1.4 %collective-permute-start.5 = (bf16[256,128]{1,0:T(8,128)(2,1)S(1)}, bf16[256,128]{1,0:T(8,128)(2,1)S(1)}, u32[]{:S(2)}, u32[]{:S(2)}) collective-permute-start(bf16[256,128]{1,0:T(8,128)(2,1)S(1)} %add_convert_fusion.here), channel_id=1, source_target_pairs={{0,64},{16,80},{32,96},{48,112},{64,0},{80,16},{96,32},{112,48},{1... | collective-permute-start | bytes 196616 | tf_op jit(solution)/shard_map/ppermute | solution.py:267
  46.4 1.7 %shard_map.117 = (f32[2,512,128]{2,1,0:T(8,128)S(1)}, bf16[256,4096]{1,0:T(8,128)(2,1)S(1)}) custom-call(s32[1]{0:T(128)} %bitcast.index, bf16[256,2,256]{2,1,0:T(2,128)(2,1)} %near_hbm.1, bf16[512,256]{1,0:T(8,128)(2,1)S(1)} %get-tuple-element.31.fh.f, bf16[256,4096]{1,0:T(8,128)(2,1)} %w_hbm.1), custom_call_target="tpu_custom_call" | custom-call | flops 134217728 | bytes 2097152 | tf_op jit(solution)/shard_map/pallas_call | solution.py:352
  48.1 2.5 %collective-permute-done.5.there = bf16[256,128]{1,0:T(8,128)(2,1)S(1)} collective-permute-done((bf16[256,128]{1,0:T(8,128)(2,1)S(1)}, bf16[256,128]{1,0:T(8,128)(2,1)S(1)}, u32[]{:S(2)}, u32[]{:S(2)}) %collective-permute-start.5) | collective-permute-done | bytes 65568 | tf_op jit(solution)/shard_map/ppermute | solution.py:267
  50.6 2.8 %all-to-all-done.1.arrived = bf16[16,48,128]{2,1,0:T(8,128)(2,1)S(1)} async-done(((bf16[16,48,128]{2,1,0:T(8,128)(2,1)}), bf16[16,48,128]{2,1,0:T(8,128)(2,1)S(1)}, u32[]{:S(2)}, u32[]{:S(2)}) %all-to-all-start.1) | async-done | bytes 196640 | tf_op jit(solution)/shard_map/all_to_all | solution.py:263
  53.5 0.9 %shard_map.118 = (f32[2,16,128]{2,1,0:T(8,128)S(1)}, f32[2,16,128]{2,1,0:T(8,128)S(1)}) custom-call(s32[1]{0:T(128)} %bitcast.index, bf16[16,48,128]{2,1,0:T(8,128)(2,1)S(1)} %all-to-all-done.1.arrived, bf16[256,128]{1,0:T(8,128)(2,1)S(1)} %add_convert_fusion.here, bf16[256,128]{1,0:T(8,128)(2,1)S(1)} %collective-permute-done.5.there, ...), custom_call_target="tpu_custom_call" | custom-call | flops 268435456 | bytes 4194304 | tf_op jit(solution)/shard_map/pallas_call | solution.py:362
  54.4 0.2 collective-permute-start.6
  54.6 1.1 %collective-permute-done.6.came = f32[2,16,128]{2,1,0:T(8,128)S(1)} collective-permute-done((f32[2,16,128]{2,1,0:T(8,128)S(1)}, f32[2,16,128]{2,1,0:T(8,128)S(1)}, u32[]{:S(2)}, u32[]{:S(2)}) %collective-permute-start.6) | collective-permute-done | bytes 16416 | tf_op jit(solution)/shard_map/ppermute | solution.py:267
  55.7 0.9 %shard_map.119 = (bf16[16,16,256]{2,1,0:T(8,128)(2,1)S(1)}, bf16[16,256]{1,0:T(8,128)(2,1)}) custom-call(s32[1]{0:T(128)} %bitcast.index, f32[2,16,128]{2,1,0:T(8,128)S(1)} %get-tuple-element.44.keep, f32[2,16,128]{2,1,0:T(8,128)S(1)} %collective-permute-done.6.came, bf16[16,256]{1,0:T(8,128)(2,1)S(1)} %get-tuple-element.46.gate_two, ...), custom_call_target="tpu_custom_call" | custom-call | flops 67108864 | bytes 1048576 | tf_op jit(solution)/shard_map/pallas_call | solution.py:374
  56.5 11.5 %all_to_all.15.arrived = bf16[16,16,256]{2,1,0:T(8,128)(2,1)S(1)} all-to-all(bf16[16,16,256]{2,1,0:T(8,128)(2,1)S(1)} %get-tuple-element.48), channel_id=1, replica_groups=mesh['ctx'=16,'chan'=16] {'chan'}, dimensions={0} | all-to-all | bytes 262144 | tf_op jit(solution)/shard_map/all_to_all | solution.py:263
  68.1 0.6 shard_map.120
  (3 shorter events, 0.1 us)
Async XLA Ops:
  0.6 10.5 %collective-permute-start = (bf16[256,2,256]{2,1,0:T(2,128)(2,1)}, bf16[256,2,256]{2,1,0:T(2,128)(2,1)S(1)}, u32[]{:S(2)}, u32[]{:S(2)}) collective-permute-start(bf16[256,2,256]{2,1,0:T(2,128)(2,1)} %refs_1_.1), channel_id=1, source_target_pairs={{16,0},{32,16},{48,32},{64,48},{80,64},{96,80},{112,96},{128,112},... | collective-permute-start | bytes 786440 | tf_op jit(solution)/shard_map/ppermute | solution.py:286
  12.5 0.7 %copy-start = (bf16[3,256,256]{2,1,0:T(8,128)(2,1)}, bf16[3,256,256]{2,1,0:T(8,128)(2,1)S(1)}, u32[]{:S(2)}) copy-start(bf16[3,256,256]{2,1,0:T(8,128)(2,1)S(1)} %get-tuple-element.35.rows) | copy-start | bytes 1179652
  13.3 11.9 %collective-permute-start.2 = (f32[256,128]{1,0:T(8,128)S(1)}, f32[256,128]{1,0:T(8,128)S(1)}, u32[]{:S(2)}, u32[]{:S(2)}) collective-permute-start(f32[256,128]{1,0:T(8,128)S(1)} %get-tuple-element.40), channel_id=1, source_target_pairs={{0,16},{16,0},{32,48},{48,32},{64,80},{80,64},{96,112},{112,96},{1... | collective-permute-start | bytes 393224 | tf_op jit(solution)/shard_map/ppermute | solution.py:267
  13.3 17.5 %all-to-all-start = ((bf16[16,16,256]{2,1,0:T(8,128)(2,1)}), bf16[16,16,256]{2,1,0:T(8,128)(2,1)S(1)}, u32[]{:S(2)}, u32[]{:S(2)}) async-start(bf16[16,16,256]{2,1,0:T(8,128)(2,1)} %get-tuple-element.26), calls=%async_computation | async-start | bytes 262144 | tf_op jit(solution)/shard_map/all_to_all | solution.py:263
  22.4 1.0 %copy-start.1 = (bf16[3,256,256]{2,1,0:T(8,128)(2,1)S(1)}, bf16[3,256,256]{2,1,0:T(8,128)(2,1)}, u32[]{:S(2)}) copy-start(bf16[3,256,256]{2,1,0:T(8,128)(2,1)} %copy-done) | copy-start | bytes 1179652
  24.3 6.6 %collective-permute-start.1 = (f32[256,128]{1,0:T(8,128)S(1)}, f32[256,128]{1,0:T(8,128)S(1)}, u32[]{:S(2)}, u32[]{:S(2)}) collective-permute-start(f32[256,128]{1,0:T(8,128)S(1)} %get-tuple-element.37), channel_id=1, source_target_pairs={{0,16},{16,0},{32,48},{48,32},{64,80},{80,64},{96,112},{112,96},{1... | collective-permute-start | bytes 393224 | tf_op jit(solution)/shard_map/ppermute | solution.py:267
  25.2 8.8 %collective-permute-start.3 = (bf16[256,128]{1,0:T(8,128)(2,1)S(1)}, bf16[256,128]{1,0:T(8,128)(2,1)S(1)}, u32[]{:S(2)}, u32[]{:S(2)}) collective-permute-start(bf16[256,128]{1,0:T(8,128)(2,1)S(1)} %add_convert_fusion.2), channel_id=1, source_target_pairs={{0,32},{16,48},{32,0},{48,16},{64,96},{80,112},{96,64},{112,80},{1... | collective-permute-start | bytes 196616 | tf_op jit(solution)/shard_map/ppermute | solution.py:267
  34.0 10.9 %collective-permute-start.4 = (bf16[256,128]{1,0:T(8,128)(2,1)S(1)}, bf16[256,128]{1,0:T(8,128)(2,1)S(1)}, u32[]{:S(2)}, u32[]{:S(2)}) collective-permute-start(bf16[256,128]{1,0:T(8,128)(2,1)S(1)} %add_convert_fusion.1), channel_id=1, source_target_pairs={{0,128},{16,144},{32,160},{48,176},{64,192},{80,208},{96,224},{112... | collective-permute-start | bytes 196616 | tf_op jit(solution)/shard_map/ppermute | solution.py:267
  36.9 16.6 %all-to-all-start.1 = ((bf16[16,48,128]{2,1,0:T(8,128)(2,1)}), bf16[16,48,128]{2,1,0:T(8,128)(2,1)S(1)}, u32[]{:S(2)}, u32[]{:S(2)}) async-start(bf16[16,48,128]{2,1,0:T(8,128)(2,1)} %get-tuple-element.41), calls=%async_computation.1 | async-start | bytes 393216 | tf_op jit(solution)/shard_map/all_to_all | solution.py:263
  44.9 5.7 %collective-permute-start.5 = (bf16[256,128]{1,0:T(8,128)(2,1)S(1)}, bf16[256,128]{1,0:T(8,128)(2,1)S(1)}, u32[]{:S(2)}, u32[]{:S(2)}) collective-permute-start(bf16[256,128]{1,0:T(8,128)(2,1)S(1)} %add_convert_fusion.here), channel_id=1, source_target_pairs={{0,64},{16,80},{32,96},{48,112},{64,0},{80,16},{96,32},{112,48},{1... | collective-permute-start | bytes 196616 | tf_op jit(solution)/shard_map/ppermute | solution.py:267
  54.4 1.3 %collective-permute-start.6 = (f32[2,16,128]{2,1,0:T(8,128)S(1)}, f32[2,16,128]{2,1,0:T(8,128)S(1)}, u32[]{:S(2)}, u32[]{:S(2)}) collective-permute-start(f32[2,16,128]{2,1,0:T(8,128)S(1)} %get-tuple-element.45), channel_id=1, source_target_pairs={{0,16},{16,0},{32,48},{48,32},{64,80},{80,64},{96,112},{112,96},{1... | collective-permute-start | bytes 49160 | tf_op jit(solution)/shard_map/ppermute | solution.py:267
